TPU v7x, 512 devices: a whole 4x8x8 slice. The times are simulated.
512 devices in a mesh: ta: 64 (over z, x, core), pa: 8 (over y).
Axes of the slice: x: 4, y: 8, z: 8, core: 2. Of those that a mesh axis runs over, the one named last changes fastest.
Arguments:
- occupied_orbitals: bfloat16 [4096, 512], P('pa'), may hold values from -3 to 3
- virtual_orbitals: bfloat16 [4096, 1536], P('pa'), may hold values from -2.5 to 2.5
- occupied_gaps: float32 [512], replicated, may hold values from 0.05 to 2
- virtual_gaps: float32 [1536], replicated, may hold values from 0.05 to 2
- tile_columns: int32 [32, 8], replicated, may hold values from 0 to 31, as said below
- probe_vectors: bfloat16 [32, 4096], P(None, 'ta'), may hold values from -0.1875 to 0.1875
Outputs:
- response: float32 [64, 32, 4096], P('ta', None, 'pa')
Inputs may be any that keep to these rules, and one draw needn't show every extreme that they name: `tile_columns`: each row block lists 8 different column blocks, and every column block is listed by some row block.
All inputs are finite; a program needn't handle non-finite values.
Results may differ from a plain program's by a relative error of at most 0.00083.
Values may be sent and summed in bfloat16 or wider, within the bound.
A program may use at most 64 MiB of HBM per device.

v0:
```python
import jax
import jax.numpy as jnp
from jax import lax
from jax.sharding import PartitionSpec as P

BLK = 128
NT = 32
NVEC = 32
F_DEV = 1


def spread(value, axis, source):
    kept = jnp.where(lax.axis_index(axis) == source, value, 0).astype(value.dtype)
    return lax.psum(kept, axis)


def quadrature_grids(count_times, count_freqs):
    low_time = jnp.log(jnp.float32(0.05))
    high_time = jnp.log(jnp.float32(8.0))
    time_place = (jnp.arange(count_times, dtype=jnp.float32) + 0.5) / count_times
    times_grid = jnp.exp(low_time + (high_time - low_time) * time_place)
    weights_grid = times_grid * (high_time - low_time) / count_times
    low_freq = jnp.log(jnp.float32(0.05))
    high_freq = jnp.log(jnp.float32(20.0))
    freq_place = (jnp.arange(count_freqs, dtype=jnp.float32) + 0.5) / count_freqs
    freqs_grid = jnp.exp(low_freq + (high_freq - low_freq) * freq_place)
    cosine_table = 2.0 * weights_grid[None, :] * jnp.cos(freqs_grid[:, None] * times_grid[None, :])
    return (times_grid, cosine_table)


def shards(
    occupied_orbitals, virtual_orbitals, occupied_gaps, virtual_gaps, tile_columns, probe_vectors
):
    count_ta = lax.axis_size("ta")
    panel_rows = occupied_orbitals.shape[0]
    slice_width = probe_vectors.shape[1]
    occ_count = occupied_orbitals.shape[1]
    block_count = panel_rows // BLK
    first_block = lax.axis_index("pa") * block_count
    times_grid, cosine_table = quadrature_grids(NT, F_DEV * count_ta)
    occ_weights = jnp.exp(-times_grid[:, None] * occupied_gaps[None, :])
    virt_weights = jnp.exp(-times_grid[:, None] * virtual_gaps[None, :])
    start_terms = jnp.zeros((NT, NVEC, panel_rows), jnp.float32)
    slice_start = lax.axis_index("ta") * slice_width
    owner_panel = slice_start // panel_rows
    offset_rows = slice_start % panel_rows
    local_part = jnp.concatenate(
        [
            lax.dynamic_slice_in_dim(occupied_orbitals, offset_rows, slice_width, 0),
            lax.dynamic_slice_in_dim(virtual_orbitals, offset_rows, slice_width, 0),
        ],
        axis=1,
    )
    column_part = spread(local_part, "pa", owner_panel)
    column_occ = column_part[:, :occ_count]
    column_virt = column_part[:, occ_count:]
    scaled_occ = (column_occ[None].astype(jnp.float32) * occ_weights[:, None, :]).astype(
        jnp.bfloat16
    )
    scaled_virt = (column_virt[None].astype(jnp.float32) * virt_weights[:, None, :]).astype(
        jnp.bfloat16
    )
    panel_tiles = lax.dynamic_slice_in_dim(tile_columns, first_block, block_count, 0)
    column_blocks = (slice_start + jnp.arange(slice_width, dtype=jnp.int32)) // BLK
    present = jnp.any(panel_tiles[:, :, None] == column_blocks[None, None, :], axis=1)
    column_mask = present.astype(jnp.float32)
    empty_terms = jnp.zeros((NT, NVEC, BLK), jnp.float32)

    def block_result(which_block):
        row_occ = lax.dynamic_slice_in_dim(occupied_orbitals, which_block * BLK, BLK, 0)
        row_virt = lax.dynamic_slice_in_dim(virtual_orbitals, which_block * BLK, BLK, 0)
        green_occ = jnp.einsum(
            "tci,ri->tcr", scaled_occ, row_occ, preferred_element_type=jnp.float32
        )
        green_virt = jnp.einsum(
            "tca,ra->tcr", scaled_virt, row_virt, preferred_element_type=jnp.float32
        )
        mask_row = column_mask[which_block]
        polar = (green_occ * green_virt * mask_row[None, :, None]).astype(jnp.bfloat16)
        return jnp.einsum("vc,tcr->tvr", probe_vectors, polar, preferred_element_type=jnp.float32)

    def visit_block(time_terms, which_block):
        block_terms = lax.cond(
            jnp.any(present[which_block]),
            block_result,
            lambda skipped_block: empty_terms,
            which_block,
        )
        return (
            lax.dynamic_update_slice_in_dim(time_terms, block_terms, which_block * BLK, 2),
            None,
        )

    time_terms, _ = lax.scan(visit_block, start_terms, jnp.arange(block_count, dtype=jnp.int32))
    highest = lax.Precision.HIGHEST
    partial_response = jnp.einsum("kt,tvr->kvr", cosine_table, time_terms, precision=highest)
    response = lax.psum_scatter(partial_response, "ta", scatter_dimension=0, tiled=True)
    return response


def solution(mesh):
    placed = (P("pa", None), P("pa", None), P(), P(), P(), P(None, "ta"))
    return jax.shard_map(
        shards, mesh=mesh, in_specs=placed, out_specs=P("ta", None, "pa"), check_vma=False
    )
```

profile of v0, /device:TPU:1, one launch (start us, length us, event | category | flops | bytes accessed | tf_op | source)
XLA Modules:
  0.0 351.1 jit_solution(4372442676124110581)
XLA Ops:
  6.5 0.0 copy-start
  6.5 0.0 all-reduce.3.cloned.1.call-start
  6.5 1.0 constant_dynamic-slice_fusion.1
  7.5 0.0 copy-start.1
  7.5 0.9 constant_dynamic-slice_fusion.2
  8.4 0.7 maximum_select_fusion
  9.1 0.0 all-reduce.3.cloned.1.call-update
  9.1 0.0 reduce-scatter.4.cloned.1.call-start
  9.2 0.6 add_exponential_fusion.1
  9.8 0.0 copy-done
  9.8 0.1 constant_dynamic-slice_fusion.3
  9.9 0.1 copy.13
  10.0 0.6 compare_reduce_fusion
  10.6 1.5 multiply_exponential_fusion
  12.1 0.5 add_exponential_fusion
  12.6 0.6 convert_element_type.32
  13.2 1.4 multiply_exponential_fusion.1
  14.6 73.4 %all-reduce.3.cloned.1.call-done = bf16[64,2048]{1,0:T(8,128)(2,1)} async-done(((bf16[64,2048]{1,0:T(8,128)(2,1)}), bf16[64,2048]{1,0:T(8,128)(2,1)}) %all-reduce.3.cloned.1.call-update) | async-done | bytes 262160 | tf_op jit(solution)/shard_map/psum | solution.py:14
  88.0 1.0 slice_convert_fusion
  88.9 1.5 slice_convert_fusion.1
  90.5 0.5 iota.28
  91.0 1.6 broadcast_in_dim.7.clone
  92.6 0.0 copy-done.1
  92.6 56.1 %while.11 = (s32[]{:T(128)}, f32[32,32,512]{2,0,1:T(8,128)}, s32[4]{0:T(128)}, pred[4,64]{1,0:T(4,128)(4,1)}, bf16[512,512]{1,0:T(8,128)(2,1)}, /*index=5*/bf16[...) while((s32[]{:T(128)}, f32[32,32,512]{2,0,1:T(8,128)}, ...), condition=%wide.region_6.7_spmd.clone, body=%wide.region_2.6_spmd.clone.sunk | while | flops 1099694208 | bytes 21763300 | solution.py:94
  92.6 1.3 dynamic_slice.49
  95.9 1.3 dynamic-slice_reduce_fusion.2
  97.7 5.4 %multiply_convert_fusion.5 = bf16[32,64,1536]{2,1,0:T(8,128)(2,1)} fusion(f32[32,1536]{1,0:T(8,128)} %get-tuple-element.256, f32[64,1536]{1,0:T(8,128)S(1)} %get-tuple-element.257), kind=kLoop, calls=%fused_computation.19.clone.1 | loop fusion | flops 6291456 | bytes 6881280 | tf_op jit(solution)/shard_map/convert_element_type | solution.py:60
  103.1 1.5 multiply_convert_fusion.4
  104.7 0.1 conditional.3
  104.7 0.1 broadcast_in_dim.1
  105.4 1.1 copy_dynamic-update-slice_fusion.2
  106.6 1.3 dynamic_slice.49
  109.9 1.3 dynamic-slice_reduce_fusion.2
  111.8 5.4 %multiply_convert_fusion.5 = bf16[32,64,1536]{2,1,0:T(8,128)(2,1)} fusion(f32[32,1536]{1,0:T(8,128)} %get-tuple-element.256, f32[64,1536]{1,0:T(8,128)S(1)} %get-tuple-element.257), kind=kLoop, calls=%fused_computation.19.clone.1 | loop fusion | flops 6291456 | bytes 6881280 | tf_op jit(solution)/shard_map/convert_element_type | solution.py:60
  117.2 1.5 multiply_convert_fusion.4
  118.7 0.1 conditional.3
  118.7 0.1 broadcast_in_dim.1
  119.5 1.1 copy_dynamic-update-slice_fusion.2
  120.6 1.3 dynamic_slice.49
  124.0 1.3 dynamic-slice_reduce_fusion.2
  125.8 5.4 %multiply_convert_fusion.5 = bf16[32,64,1536]{2,1,0:T(8,128)(2,1)} fusion(f32[32,1536]{1,0:T(8,128)} %get-tuple-element.256, f32[64,1536]{1,0:T(8,128)S(1)} %get-tuple-element.257), kind=kLoop, calls=%fused_computation.19.clone.1 | loop fusion | flops 6291456 | bytes 6881280 | tf_op jit(solution)/shard_map/convert_element_type | solution.py:60
  131.2 1.5 multiply_convert_fusion.4
  132.7 0.1 conditional.3
  132.7 0.1 broadcast_in_dim.1
  133.5 1.1 copy_dynamic-update-slice_fusion.2
  134.7 1.3 dynamic_slice.49
  138.0 1.3 dynamic-slice_reduce_fusion.2
  139.8 5.4 %multiply_convert_fusion.5 = bf16[32,64,1536]{2,1,0:T(8,128)(2,1)} fusion(f32[32,1536]{1,0:T(8,128)} %get-tuple-element.256, f32[64,1536]{1,0:T(8,128)S(1)} %get-tuple-element.257), kind=kLoop, calls=%fused_computation.19.clone.1 | loop fusion | flops 6291456 | bytes 6881280 | tf_op jit(solution)/shard_map/convert_element_type | solution.py:60
  145.2 1.5 multiply_convert_fusion.4
  146.8 0.1 conditional.3
  146.8 0.1 broadcast_in_dim.1
  147.5 1.2 copy_dynamic-update-slice_fusion.2
  148.7 5.3 %fusion.22 = f32[64,32,512]{2,0,1:T(8,128)S(1)} fusion(f32[32,32,512]{2,0,1:T(8,128)} %get-tuple-element.81, f32[32]{0:T(128)} %get-tuple-element.137, f32[64]{0:T(128)} %add_exponential_fusion, f32[32]{0:T(128)} %get-tuple-element.138), kind=kOutput, calls=%fused_computation.28 | convolution fusion | flops 402657280 | bytes 6291968 | tf_op jit(solution)/shard_map/kt,tvr->kvr/dot_general | solution.py:96
  154.0 4.4 %copy.15 = f32[64,32,512]{2,1,0:T(8,128)} copy(f32[64,32,512]{2,0,1:T(8,128)S(1)} %fusion.22) | data formatting | bytes 8388608 | tf_op jit(solution)/shard_map/kt,tvr->kvr/dot_general | solution.py:96
  158.4 0.0 reduce-scatter.4.cloned.1.call-update
  158.4 185.8 %reduce-scatter.4.cloned.1.call-done = f32[1,32,512]{2,1,0:T(8,128)} async-done(((f32[64,32,512]{2,1,0:T(8,128)}), f32[1,32,512]{2,1,0:T(8,128)}) %reduce-scatter.4.cloned.1.call-update) | async-done | bytes 65552
  (2 shorter events, 0.0 us)
Async XLA Ops:
  6.5 3.3 copy-start
  6.5 81.5 %all-reduce.3.cloned.1.call-start = ((), (), s32[]{:S(2)}) async-start(), calls=%async_computation.1 | async-start | bytes 524288 | tf_op jit(solution)/shard_map/psum | solution.py:14
  7.5 85.1 %copy-start.1 = (bf16[32,64]{1,0:T(8,128)(2,1)S(1)}, bf16[32,64]{1,0:T(8,128)(2,1)}, u32[]{:S(2)}) copy-start(bf16[32,64]{1,0:T(8,128)(2,1)} %param.15) | copy-start | bytes 12292
  9.1 335.1 %reduce-scatter.4.cloned.1.call-start = ((), (), s32[]{:S(2)}) async-start(), calls=%async_computation.2 | async-start | bytes 4259840
Sparse Core Ops, SparseCore 0:
  9.6 78.3 all-reduce.2
  158.5 185.6 reduce-scatter.3
where the time goes:
time: 356 us; the launch traced here: 351 us
  waiting for transfers between devices  259 us (73%)
  other arithmetic  41.2 us (12%)
  local copies, waits for them, and re-layouts  18.3 us (5%)
  loops' own time  13.6 us (4%)
  between operations  13.4 us (4%)
  matrix products  5.32 us (1%)
    unnamed x3, waiting for transfers between devices  186 us
    psum x1, waiting for transfers between devices, spread(): return lax.psum(kept, axis)  73.4 us
    convert_element_type x4, other arithmetic, shards(): (column_virt[None].astype(jnp.float32) * virt_weights[:, None, :]).astype...  21.5 us
    another operation x1, loops' own time, shards(): lax.scan(visit_block, start_terms, jnp.arange(block_count, dtype=jnp.int32))  13.5 us
  transfers between devices with their start and end apart: 2, of which 2 were waited for; matrix products, arithmetic and copies ran while one was open for 2% of the time, Pallas kernels for 0%

commit v1 on v0

v1 whole, which is shorter than its diff:
```python
import functools

import jax
import jax.numpy as jnp
import numpy as np
from jax import lax
from jax.experimental import pallas as pl
from jax.experimental.pallas import tpu as pltpu
from jax.sharding import PartitionSpec as P

MESH = pl.DeviceIdType.MESH
NT = 32
NVEC = 32
BLK = 128
NZ = 8
NX = 4
NY = 8
COLS = 16
CHIP_COLS = NY * COLS
ROWS = 256
LINK = jnp.bfloat16


def quadrature_grids(count_times, count_freqs):
    place = (np.arange(count_times) + 0.5) / count_times
    times = np.exp(np.log(0.05) + np.log(160.0) * place)
    freqs = np.exp(np.log(0.05) + np.log(400.0) * (np.arange(count_freqs) + 0.5) / count_freqs)
    table = 2.0 * times[None, :] * np.log(160.0) / count_times * np.cos(freqs[:, None] * times[None, :])
    return times.astype(np.float32), table.astype(np.float32)


def owner_block(x):
    high = jnp.where((x == 1) | (x == 2), 1, 0)
    low = jnp.where(x >= 2, 1, 0)
    return 2 * high + low


def kernel(
    occ_hbm, virt_hbm, ogap_ref, vgap_ref, tiles_ref, probe_ref, times_ref, table_ref, out_ref,
    points, r_occ, r_virt, weights, s_occ, s_virt, polar, padded, probes, picked_out, picked_in, left,
    keep, x1_out, x1_in, x2_out, x2_in, sums, zs_out, zs_in, trans, za_in, xa_out, whole,
    local_sem, y_send, y_recv, f_send, f_recv, p_send, p_recv, ps_send, ps_recv,
    x_send, x_recv, zs_send, zs_recv, za_send, za_recv, xa_send, xa_recv,
):
    ta = lax.axis_index("ta")
    y = lax.axis_index("pa")
    z = ta // 8
    e = ta % 8
    x = e // 2
    c = e % 2
    n_occ = occ_hbm.shape[1]
    n_virt = virt_hbm.shape[1]
    h_occ, h_virt = n_occ // 2, n_virt // 2

    def at(z_, e_, y_):
        return (z_ * 8 + e_, y_)

    barrier = pltpu.get_barrier_semaphore()
    for d in range(1, 8):
        for who in (at(lax.rem(z + d, NZ), e, y), at(z, lax.rem(e + d, 8), y)):
            pl.semaphore_signal(barrier, inc=1, device_id=who, device_id_type=MESH)
    for d in (1, 2, 6, 7):
        pl.semaphore_signal(
            barrier, inc=1, device_id=at(z, e, lax.rem(y + d, NY)), device_id_type=MESH
        )

    first = pl.multiple_of(x * 128 + z * COLS, COLS)
    mine = pl.ds(first, COLS)
    row0 = pl.multiple_of(c * ROWS, ROWS)
    own_copies = []
    for h in range(2):
        own_copies += [
            pltpu.make_async_copy(
                occ_hbm.at[mine, h * h_occ:(h + 1) * h_occ], points.at[0, h, :, :h_occ],
                local_sem.at[h]),
            pltpu.make_async_copy(
                virt_hbm.at[mine, h * h_virt:(h + 1) * h_virt], points.at[0, h, :, h_occ:],
                local_sem.at[2 + h]),
        ]
    row_copies = [
        pltpu.make_async_copy(occ_hbm.at[pl.ds(row0, ROWS), :], r_occ, local_sem.at[4]),
        pltpu.make_async_copy(virt_hbm.at[pl.ds(row0, ROWS), :], r_virt, local_sem.at[5]),
    ]
    for copy in own_copies + row_copies:
        copy.start()
    padded[:, :64] = probe_ref[...]
    padded[:, 64:] = jnp.zeros((NVEC, 64), jnp.bfloat16)
    for copy in own_copies:
        copy.wait()
    pl.semaphore_wait(barrier, 18)

    sends = []

    def remote(src, dst, send, recv, who):
        copy = pltpu.make_async_remote_copy(
            src_ref=src, dst_ref=dst, send_sem=send, recv_sem=recv, device_id=who,
            device_id_type=MESH,
        )
        copy.start()
        sends.append(copy)
        return copy

    def along_y(source, target, step, sem, part=slice(None)):
        return remote(
            points.at[source, c, :, part], points.at[target, c, :, part], y_send.at[sem],
            y_recv.at[sem], at(z, e, lax.rem(y + step + NY, NY)),
        )

    gathers = {
        2: along_y(0, 2, -2, 2), 6: along_y(0, 6, 2, 6), 1: along_y(0, 1, -1, 1),
        7: along_y(0, 7, 1, 7),
    }
    sibling = at(z, x * 2 + 1 - c, y)
    probe_copies = []
    for d in range(1, 8):
        probe_copies.append(
            remote(padded, probes.at[z], p_send.at[d], p_recv.at[d],
                   at(lax.rem(z + d, NZ), e, y))
        )
    probes[z] = padded[...]

    weights[:, :n_occ] = jnp.exp(-times_ref[...] * ogap_ref[...])
    for j in range(n_virt // 128):
        weights[:, n_occ + j * 128:n_occ + (j + 1) * 128] = jnp.exp(
            -times_ref[...] * vgap_ref[j:j + 1, :]
        )

    tiles = tiles_ref[...]
    lane32 = lax.broadcasted_iota(jnp.int32, (1, 32), 1)
    lane_r = lax.broadcasted_iota(jnp.int32, (1, ROWS), 1)
    row_block = y * 4 + c * 2
    for copy in row_copies:
        copy.wait()

    def chunk(d, t_half):
        column_block = lax.rem(y + d, NY) * 4 + x
        hit = jnp.max(jnp.where(tiles == column_block, 1.0, 0.0), axis=0, keepdims=True)
        first_hit = jnp.sum(jnp.where(lane32 == row_block, hit, 0.0), axis=1, keepdims=True)
        second_hit = jnp.sum(jnp.where(lane32 == row_block + 1, hit, 0.0), axis=1, keepdims=True)
        mask = jnp.where(lane_r < BLK, first_hit, second_hit)
        for h in range(2):
            xo = points[d, h, :, :h_occ].astype(jnp.float32)
            xv = points[d, h, :, h_occ:].astype(jnp.float32)
            occ_lanes = slice(h * h_occ, (h + 1) * h_occ)
            virt_lanes = slice(h * h_virt, (h + 1) * h_virt)
            for t in range(16):
                row = t_half * 16 + t
                s_occ[t_half, t * COLS:(t + 1) * COLS, occ_lanes] = (
                    xo * weights[row:row + 1, occ_lanes]
                ).astype(jnp.bfloat16)
                s_virt[t_half, t * COLS:(t + 1) * COLS, virt_lanes] = (
                    xv * weights[row:row + 1, n_occ + h * h_virt:n_occ + (h + 1) * h_virt]
                ).astype(jnp.bfloat16)
        dims = (((1,), (1,)), ((), ()))
        green_occ = lax.dot_general(
            s_occ[t_half], r_occ[...], dims, preferred_element_type=jnp.float32
        )
        green_virt = lax.dot_general(
            s_virt[t_half], r_virt[...], dims, preferred_element_type=jnp.float32
        )
        value = (green_occ * green_virt * mask).astype(jnp.bfloat16)
        polar[t_half * 16:(t_half + 1) * 16, d * COLS:(d + 1) * COLS, :] = value.reshape(
            16, COLS, ROWS
        )

    siblings = {}

    def forward(d):
        siblings[d] = remote(
            points.at[d, c], points.at[d, c], f_send.at[d], f_recv.at[d], sibling
        )

    def both(d):
        siblings[d].wait_recv()
        chunk(d, 0)
        chunk(d, 1)

    chunk(0, 0)
    chunk(0, 1)
    quarter = (h_occ + h_virt) // 2
    gathers[2].wait_recv()
    gathers[3] = along_y(2, 3, -1, 3)
    gathers[4] = along_y(2, 4, -2, 4, slice(0, quarter))
    gathers[6].wait_recv()
    gathers[5] = along_y(6, 5, 1, 5)
    gathers[8] = along_y(6, 4, 2, 8, slice(quarter, 2 * quarter))
    for d in (2, 6):
        forward(d)
    for d in (1, 7):
        gathers[d].wait_recv()
        forward(d)
    both(1)
    both(7)
    for d in (3, 5):
        gathers[d].wait_recv()
        forward(d)
    both(2)
    both(6)
    gathers[4].wait_recv()
    gathers[8].wait_recv()
    forward(4)

    for copy in probe_copies:
        copy.wait_recv()
    lane = lax.broadcasted_iota(jnp.int32, (128, CHIP_COLS), 1)
    source = lax.broadcasted_iota(jnp.int32, (128, CHIP_COLS), 0)
    matched = source == lax.rem(z, 4) * COLS + lane % COLS
    gathered = jnp.zeros((NVEC, CHIP_COLS), jnp.float32)
    for q in range(NY):
        slot = lax.rem(q - y + NY, NY)
        pick = jnp.where((lane // COLS == slot) & matched, 1.0, 0.0).astype(jnp.bfloat16)
        gathered += jnp.dot(probes[q], pick, preferred_element_type=jnp.float32)
    picked_out[...] = gathered.astype(jnp.bfloat16)
    probe_forward = remote(picked_out, picked_in, ps_send, ps_recv, sibling)
    both(3)
    both(5)
    probe_forward.wait_recv()
    gathered = jnp.where(
        z // 4 == c, picked_out[...].astype(jnp.float32), picked_in[...].astype(jnp.float32)
    )
    gathered = gathered.astype(jnp.bfloat16)
    near, far = x + 1 - 2 * lax.rem(x, 2), 3 - x
    orders = (
        (owner_block(3 - near), owner_block(near), owner_block(far), owner_block(x)),
        (owner_block(far + 1 - 2 * lax.rem(far, 2)), owner_block(far), owner_block(near),
         owner_block(x)),
    )
    to_row = lax.broadcasted_iota(jnp.int32, (NVEC, NVEC), 0)
    from_row = lax.broadcasted_iota(jnp.int32, (NVEC, NVEC), 1)
    for half, blocks in enumerate(orders):
        block = jnp.where(
            to_row < 16,
            jnp.where(to_row < 8, blocks[0], blocks[1]),
            jnp.where(to_row < 24, blocks[2], blocks[3]),
        )
        order = jnp.where(from_row == block * 8 + to_row % 8, 1.0, 0.0).astype(jnp.bfloat16)
        left[half] = jnp.dot(order, gathered, preferred_element_type=jnp.float32).astype(
            jnp.bfloat16
        )

    partners = (at(z, near * 2 + c, y), at(z, far * 2 + c, y))
    exchanges = []
    siblings[4].wait_recv()
    for half in range(2):
        chunk(4, half)
        for t in range(16):
            terms = jnp.dot(
                left[half], polar[half * 16 + t], preferred_element_type=jnp.float32
            )
            x1_out[half, t * 16:(t + 1) * 16, :] = terms[:16].astype(LINK)
            keep[half, t] = terms[16:]
        exchanges.append(
            remote(x1_out.at[half], x1_in.at[half], x_send.at[half], x_recv.at[half],
                   partners[half])
        )
    seconds = []
    for half in range(2):
        exchanges[half].wait_recv()
        for t in range(16):
            total = keep[half, t] + x1_in[half, t * 16:(t + 1) * 16, :].astype(jnp.float32)
            x2_out[half, t * 8:(t + 1) * 8, :] = total[:8].astype(LINK)
            for side in range(2):
                sums[side, (half * 16 + t) * 8:(half * 16 + t + 1) * 8, :] = total[
                    8:, side * 128:(side + 1) * 128
                ]
        seconds.append(
            remote(x2_out.at[half], x2_in.at[half], x_send.at[2 + half], x_recv.at[2 + half],
                   partners[1 - half])
        )
    for half in range(2):
        seconds[half].wait_recv()
        part = slice(half * 128, (half + 1) * 128)
        arrived = x2_in[half].astype(jnp.float32)
        for side in range(2):
            sums[side, part, :] += arrived[:, side * 128:(side + 1) * 128]

    for s in range(NZ):
        for side in range(2):
            picked = sums[side, pl.ds(s, NT, stride=8), :]
            zs_out[s, :, side * 128:(side + 1) * 128] = picked
    reduces = []
    for d in (4, 3, 5, 2, 6, 1, 7):
        to = lax.rem(z + d, NZ)
        reduces.append(
            remote(zs_out.at[to], zs_in.at[d], zs_send.at[d], zs_recv.at[d], at(to, e, y))
        )
    total = zs_out[z]
    for copy, d in reversed(list(zip(reduces, (4, 3, 5, 2, 6, 1, 7)))):
        copy.wait_recv()
        total += zs_in[d]

    result = jnp.dot(
        table_ref[...], total, preferred_element_type=jnp.float32,
        precision=lax.Precision.HIGHEST,
    )
    for side in range(2):
        trans[:, side] = result[:, side * 128:(side + 1) * 128].reshape(NZ, 8, 128)
    slot = pl.ds(pl.multiple_of(z * 8, 8), 8)
    moves = []
    for d in (4, 3, 5, 2, 6, 1, 7):
        to = lax.rem(z + d, NZ)
        moves.append(
            remote(trans.at[to], za_in.at[:, slot, :], za_send.at[d], za_recv.at[d],
                   at(to, e, y))
        )
    za_in[:, slot, :] = trans[z]
    for copy in moves:
        copy.wait_recv()
    for k in range(8):
        for side in range(2):
            xa_out[k, :, side * 128:(side + 1) * 128] = za_in[side, pl.ds(k, 8, stride=8), :]
    place = (
        pl.ds(pl.multiple_of(owner_block(x) * 8, 8), 8),
        pl.ds(pl.multiple_of(c * ROWS, ROWS), ROWS),
    )
    finals = []
    for d in (4, 3, 5, 2, 6, 1, 7):
        to = lax.rem(e + d, 8)
        finals.append(
            remote(xa_out.at[to], whole.at[place], xa_send.at[d], xa_recv.at[d], at(z, to, y))
        )
    whole[place] = xa_out[e]
    for copy in finals:
        copy.wait_recv()
    out_ref[0] = whole[...]
    for copy in sends:
        copy.wait_send()


def shards(occ, virt, ogap, vgap, tiles, probe):
    times, table = quadrature_grids(NT, 64)
    n_occ, n_virt = occ.shape[1], virt.shape[1]
    n_all = n_occ + n_virt
    bf16, f32 = jnp.bfloat16, jnp.float32
    dma = pltpu.SemaphoreType.DMA
    vmem = pl.BlockSpec(memory_space=pltpu.VMEM)
    hbm = pl.BlockSpec(memory_space=pl.ANY)
    return pl.pallas_call(
        kernel,
        out_shape=jax.ShapeDtypeStruct((1, NVEC, occ.shape[0]), f32),
        in_specs=[hbm, hbm, vmem, vmem, vmem, vmem, vmem, vmem],
        out_specs=vmem,
        scratch_shapes=[
            pltpu.VMEM((NY, 2, COLS, n_all // 2), bf16),
            pltpu.VMEM((ROWS, n_occ), bf16),
            pltpu.VMEM((ROWS, n_virt), bf16),
            pltpu.VMEM((NT, n_all), f32),
            pltpu.VMEM((2, 16 * COLS, n_occ), bf16),
            pltpu.VMEM((2, 16 * COLS, n_virt), bf16),
            pltpu.VMEM((NT, CHIP_COLS, ROWS), bf16),
            pltpu.VMEM((NVEC, 128), bf16),
            pltpu.VMEM((NZ, NVEC, 128), bf16),
            pltpu.VMEM((NVEC, CHIP_COLS), bf16),
            pltpu.VMEM((NVEC, CHIP_COLS), bf16),
            pltpu.VMEM((2, NVEC, CHIP_COLS), bf16),
            pltpu.VMEM((2, 16, 16, ROWS), f32),
            pltpu.VMEM((2, 256, ROWS), LINK),
            pltpu.VMEM((2, 256, ROWS), LINK),
            pltpu.VMEM((2, 128, ROWS), LINK),
            pltpu.VMEM((2, 128, ROWS), LINK),
            pltpu.VMEM((2, NT * 8, 128), f32),
            pltpu.VMEM((NZ, NT, ROWS), f32),
            pltpu.VMEM((NZ, NT, ROWS), f32),
            pltpu.VMEM((NZ, 2, 8, 128), f32),
            pltpu.VMEM((2, NZ * 8, 128), f32),
            pltpu.VMEM((8, 8, ROWS), f32),
            pltpu.VMEM((NVEC, 2 * ROWS), f32),
            dma((6,)),
            dma((9,)), dma((9,)), dma((8,)), dma((8,)),
            dma((8,)), dma((8,)), dma, dma,
            dma((4,)), dma((4,)),
            dma((8,)), dma((8,)), dma((8,)), dma((8,)), dma((8,)), dma((8,)),
        ],
        compiler_params=pltpu.CompilerParams(collective_id=0, has_side_effects=True),
    )(
        occ, virt, ogap.reshape(1, -1), vgap.reshape(-1, 128), tiles.T, probe,
        jnp.asarray(times).reshape(NT, 1), jnp.asarray(table),
    )


def solution(mesh):
    placed = (P("pa", None), P("pa", None), P(), P(), P(), P(None, "ta"))
    return jax.shard_map(
        shards, mesh=mesh, in_specs=placed, out_specs=P("ta", None, "pa"), check_vma=False
    )
```

time: 356 us -> 54.9 us (0.15); the launches traced: 351 us -> 54.6 us
  waiting for transfers between devices: 259 us -> 0 us
  Pallas kernels: 0 us -> 53.1 us
  other arithmetic: 41.2 us -> 0 us
  local copies, waits for them, and re-layouts: 18.3 us -> 1.47 us
  loops' own time: 13.6 us -> 0 us
  between operations: 13.4 us -> 0.01 us
  matrix products: 5.32 us -> 0 us
    unnamed x3 -> x0, waiting for transfers between devices: 186 us -> none
    psum x1 -> x0, waiting for transfers between devices: 73.4 us -> none  [spread(): return lax.psum(kept, axis)]
    pallas_call x0 -> x1, Pallas kernels: none -> 53.1 us  [shards(): pl.pallas_call(kernel, out_shape=jax.ShapeDtypeStruct((1, NVEC, occ.shape...]
    convert_element_type x11 -> x0, other arithmetic: 30.8 us -> none  [the longest x4 21.5 us: shards(): (column_virt[None].astype(jnp.float32) * virt_weights[:, None, :]).astype...]
    another operation x5 -> x0, loops' own time: 13.6 us -> none  [the longest x1 13.5 us: shards(): lax.scan(visit_block, start_terms, jnp.arange(block_count, dtype=jnp.int32))]
    dynamic_slice x8 -> x0, local copies, waits for them, and re-layouts: 7 us -> none  [the longest x4 5.05 us: shards(): lax.scan(visit_block, start_terms, jnp.arange(block_count, dtype=jnp.int32))]
    reduce_or x5 -> x0, other arithmetic: 5.67 us -> none  [the longest x4 5.04 us: visit_block(): jnp.any(present[which_block])]
    dot_general x1 -> x0, matrix products: 5.32 us -> none  [shards(): jnp.einsum('kt,tvr->kvr', cosine_table, time_terms, precision=highest)]
  transfers between devices with their start and end apart: 2 -> 0, of which waited for: 2 -> 0; matrix products, arithmetic and copies ran while one was open for 2% -> 0% of each run, Pallas kernels for 0% -> 0%
where the time goes in v1:
time: 54.9 us; the launch traced here: 54.6 us
  Pallas kernels  53.1 us (97%)
  local copies, waits for them, and re-layouts  1.47 us (3%)
    pallas_call x1, Pallas kernels, shards(): pl.pallas_call(kernel, out_shape=jax.ShapeDtypeStruct((1, NVEC, occ.shape...  53.1 us
    unnamed x1, local copies, waits for them, and re-layouts  1.47 us

profile of v1, /device:TPU:1, one launch (start us, length us, event | category | flops | bytes accessed | tf_op | source)
XLA Modules:
  0.0 54.6 jit_solution(17551115818914251942)
XLA Ops:
  0.0 53.1 %shard_map.82 = f32[1,32,512]{2,1,0:T(8,128)} custom-call(bf16[512,512]{1,0:T(8,128)(2,1)} %occ_hbm.1, bf16[512,1536]{1,0:T(8,128)(2,1)} %virt_hbm.1, f32[1,512]{1,0:T(1,128)} %bitcast.5, f32[12,128]{1,0:T(8,128)} %bitcast.3, s32[8,32]{1,0:T(8,128)} %bitcast.4, bf16[32,64]{1,0:T(8,128)(2,1)} %probe_ref.1, f32[32,1]{1,0:T(8,128)} %constant.6.times_ref, ...), custom_call_target="tpu_custom_call" | custom-call | tf_op jit(solution)/shard_map/pallas_call | solution.py:338
  53.2 1.5 %copy.10 = f32[1,32,512]{2,1,0:T(8,128)} copy(f32[1,32,512]{2,1,0:T(8,128)} %shard_map.82) | data formatting | bytes 131072

commit v2 on v1

--- a/solution.py
+++ b/solution.py
@@ -11,6 +11,7 @@
 MESH = pl.DeviceIdType.MESH
 NT = 32
 NVEC = 32
+NF = 64
 BLK = 128
 NZ = 8
 NX = 4
@@ -38,9 +39,9 @@
 def kernel(
     occ_hbm, virt_hbm, ogap_ref, vgap_ref, tiles_ref, probe_ref, times_ref, table_ref, out_ref,
     points, r_occ, r_virt, weights, s_occ, s_virt, polar, padded, probes, picked_out, picked_in, left,
-    keep, x1_out, x1_in, x2_out, x2_in, sums, zs_out, zs_in, trans, za_in, xa_out, whole,
+    keep, x1_out, x1_in, x2_out, x2_in, sums, zs_out, zs_in, zs_sum, trans, arrivals,
     local_sem, y_send, y_recv, f_send, f_recv, p_send, p_recv, ps_send, ps_recv,
-    x_send, x_recv, zs_send, zs_recv, za_send, za_recv, xa_send, xa_recv,
+    x_send, x_recv, zs_send, zs_recv, out_send, out_recv,
 ):
     ta = lax.axis_index("ta")
     y = lax.axis_index("pa")
@@ -56,13 +57,14 @@
         return (z_ * 8 + e_, y_)
 
     barrier = pltpu.get_barrier_semaphore()
-    for d in range(1, 8):
-        for who in (at(lax.rem(z + d, NZ), e, y), at(z, lax.rem(e + d, 8), y)):
-            pl.semaphore_signal(barrier, inc=1, device_id=who, device_id_type=MESH)
-    for d in (1, 2, 6, 7):
-        pl.semaphore_signal(
-            barrier, inc=1, device_id=at(z, e, lax.rem(y + d, NY)), device_id_type=MESH
-        )
+    near, far = x + 1 - 2 * lax.rem(x, 2), 3 - x
+    sibling = at(z, x * 2 + 1 - c, y)
+    partners = (at(z, near * 2 + c, y), at(z, far * 2 + c, y))
+    greeted = [sibling, *partners]
+    greeted += [at(z, e, lax.rem(y + d, NY)) for d in (1, 2, 6, 7)]
+    greeted += [at(lax.rem(z + d, NZ), e, y) for d in range(1, NZ)]
+    for who in greeted:
+        pl.semaphore_signal(barrier, inc=1, device_id=who, device_id_type=MESH)
 
     first = pl.multiple_of(x * 128 + z * COLS, COLS)
     mine = pl.ds(first, COLS)
@@ -87,7 +89,7 @@
     padded[:, 64:] = jnp.zeros((NVEC, 64), jnp.bfloat16)
     for copy in own_copies:
         copy.wait()
-    pl.semaphore_wait(barrier, 18)
+    pl.semaphore_wait(barrier, len(greeted))
 
     sends = []
 
@@ -110,7 +112,6 @@
         2: along_y(0, 2, -2, 2), 6: along_y(0, 6, 2, 6), 1: along_y(0, 1, -1, 1),
         7: along_y(0, 7, 1, 7),
     }
-    sibling = at(z, x * 2 + 1 - c, y)
     probe_copies = []
     for d in range(1, 8):
         probe_copies.append(
@@ -190,12 +191,11 @@
         gathers[d].wait_recv()
         forward(d)
     both(1)
-    both(7)
     for d in (3, 5):
         gathers[d].wait_recv()
         forward(d)
+    both(7)
     both(2)
-    both(6)
     gathers[4].wait_recv()
     gathers[8].wait_recv()
     forward(4)
@@ -212,6 +212,7 @@
         gathered += jnp.dot(probes[q], pick, preferred_element_type=jnp.float32)
     picked_out[...] = gathered.astype(jnp.bfloat16)
     probe_forward = remote(picked_out, picked_in, ps_send, ps_recv, sibling)
+    both(6)
     both(3)
     both(5)
     probe_forward.wait_recv()
@@ -219,7 +220,6 @@
         z // 4 == c, picked_out[...].astype(jnp.float32), picked_in[...].astype(jnp.float32)
     )
     gathered = gathered.astype(jnp.bfloat16)
-    near, far = x + 1 - 2 * lax.rem(x, 2), 3 - x
     orders = (
         (owner_block(3 - near), owner_block(near), owner_block(far), owner_block(x)),
         (owner_block(far + 1 - 2 * lax.rem(far, 2)), owner_block(far), owner_block(near),
@@ -238,7 +238,6 @@
             jnp.bfloat16
         )
 
-    partners = (at(z, near * 2 + c, y), at(z, far * 2 + c, y))
     exchanges = []
     siblings[4].wait_recv()
     for half in range(2):
@@ -260,75 +259,83 @@
             total = keep[half, t] + x1_in[half, t * 16:(t + 1) * 16, :].astype(jnp.float32)
             x2_out[half, t * 8:(t + 1) * 8, :] = total[:8].astype(LINK)
             for side in range(2):
-                sums[side, (half * 16 + t) * 8:(half * 16 + t + 1) * 8, :] = total[
-                    8:, side * 128:(side + 1) * 128
-                ]
+                sums[side, half, t * 8:(t + 1) * 8, :] = total[8:, side * 128:(side + 1) * 128]
         seconds.append(
             remote(x2_out.at[half], x2_in.at[half], x_send.at[2 + half], x_recv.at[2 + half],
                    partners[1 - half])
         )
-    for half in range(2):
+
+    def along_z(half, source, target, step, sem):
+        return remote(source, target, zs_send.at[half, sem], zs_recv.at[half, sem],
+                      at(lax.rem(z + step + NZ, NZ), e, y))
+
+    reduces, relays = [{}, {}], []
+    for half, sign in enumerate((1, -1)):
         seconds[half].wait_recv()
-        part = slice(half * 128, (half + 1) * 128)
         arrived = x2_in[half].astype(jnp.float32)
         for side in range(2):
-            sums[side, part, :] += arrived[:, side * 128:(side + 1) * 128]
-
-    for s in range(NZ):
-        for side in range(2):
-            picked = sums[side, pl.ds(s, NT, stride=8), :]
-            zs_out[s, :, side * 128:(side + 1) * 128] = picked
-    reduces = []
-    for d in (4, 3, 5, 2, 6, 1, 7):
-        to = lax.rem(z + d, NZ)
-        reduces.append(
-            remote(zs_out.at[to], zs_in.at[d], zs_send.at[d], zs_recv.at[d], at(to, e, y))
-        )
-    total = zs_out[z]
-    for copy, d in reversed(list(zip(reduces, (4, 3, 5, 2, 6, 1, 7)))):
-        copy.wait_recv()
-        total += zs_in[d]
+            lanes = slice(side * 128, (side + 1) * 128)
+            sums[side, half] += arrived[:, lanes]
+            for s in range(NZ):
+                zs_out[half, s, :, lanes] = sums[side, half, pl.ds(s, 16, stride=8), :]
+        relays.append(
+            along_z(half, zs_out.at[half, lax.rem(z + 4, NZ)], zs_in.at[half, 4], sign, 4)
+        )
+        for d in (5, 2, 6, 1, 7):
+            reduces[half][d] = along_z(
+                half, zs_out.at[half, lax.rem(z + sign * d + NZ, NZ)], zs_in.at[half, d],
+                sign * d, d,
+            )
+    for half, sign in enumerate((1, -1)):
+        relays[half].wait_recv()
+        zs_sum[half] = zs_in[half, 4] + zs_out[half, lax.rem(z + sign * 3 + NZ, NZ)]
+        reduces[half][3] = along_z(half, zs_sum.at[half], zs_in.at[half, 3], sign * 3, 3)
+    totals = []
+    for half in range(2):
+        total = zs_out[half, z]
+        for d in (7, 1, 6, 2, 5, 3):
+            reduces[half][d].wait_recv()
+            total += zs_in[half, d]
+        totals.append(total)
 
     result = jnp.dot(
-        table_ref[...], total, preferred_element_type=jnp.float32,
+        table_ref[...], jnp.concatenate(totals, axis=0), preferred_element_type=jnp.float32,
         precision=lax.Precision.HIGHEST,
     )
     for side in range(2):
-        trans[:, side] = result[:, side * 128:(side + 1) * 128].reshape(NZ, 8, 128)
-    slot = pl.ds(pl.multiple_of(z * 8, 8), 8)
-    moves = []
-    for d in (4, 3, 5, 2, 6, 1, 7):
-        to = lax.rem(z + d, NZ)
-        moves.append(
-            remote(trans.at[to], za_in.at[:, slot, :], za_send.at[d], za_recv.at[d],
-                   at(to, e, y))
-        )
-    za_in[:, slot, :] = trans[z]
-    for copy in moves:
-        copy.wait_recv()
-    for k in range(8):
-        for side in range(2):
-            xa_out[k, :, side * 128:(side + 1) * 128] = za_in[side, pl.ds(k, 8, stride=8), :]
-    place = (
-        pl.ds(pl.multiple_of(owner_block(x) * 8, 8), 8),
-        pl.ds(pl.multiple_of(c * ROWS, ROWS), ROWS),
-    )
-    finals = []
-    for d in (4, 3, 5, 2, 6, 1, 7):
-        to = lax.rem(e + d, 8)
-        finals.append(
-            remote(xa_out.at[to], whole.at[place], xa_send.at[d], xa_recv.at[d], at(z, to, y))
-        )
-    whole[place] = xa_out[e]
-    for copy in finals:
-        copy.wait_recv()
-    out_ref[0] = whole[...]
+        trans[:, side, :] = result[:, side * 128:(side + 1) * 128]
+
+    def hand_out(step, carry):
+        to = lax.rem(ta + step, NF)
+        pltpu.make_async_remote_copy(
+            src_ref=trans.at[to], dst_ref=arrivals.at[ta], send_sem=out_send, recv_sem=out_recv,
+            device_id=(to, y), device_id_type=MESH,
+        ).start()
+        return carry
+
+    lax.fori_loop(1, NF, hand_out, 0)
+    arrivals[ta] = trans[ta]
+    everything = pltpu.make_async_remote_copy(
+        src_ref=trans.at[0:NF - 1], dst_ref=arrivals.at[0:NF - 1], send_sem=out_send,
+        recv_sem=out_recv, device_id=sibling, device_id_type=MESH,
+    )
+    everything.wait_recv()
+    for x_from in range(NX):
+        block = (0, 2, 3, 1)[x_from]
+        for c_from in range(2):
+            for side in range(2):
+                lanes = slice(c_from * ROWS + side * 128, c_from * ROWS + (side + 1) * 128)
+                for z_from in range(NZ):
+                    out_ref[0, block * 8 + z_from, lanes] = arrivals[
+                        z_from * 8 + x_from * 2 + c_from, side
+                    ]
+    everything.wait_send()
     for copy in sends:
         copy.wait_send()
 
 
 def shards(occ, virt, ogap, vgap, tiles, probe):
-    times, table = quadrature_grids(NT, 64)
+    times, table = quadrature_grids(NT, NF)
     n_occ, n_virt = occ.shape[1], virt.shape[1]
     n_all = n_occ + n_virt
     bf16, f32 = jnp.bfloat16, jnp.float32
@@ -358,18 +365,17 @@
             pltpu.VMEM((2, 256, ROWS), LINK),
             pltpu.VMEM((2, 128, ROWS), LINK),
             pltpu.VMEM((2, 128, ROWS), LINK),
-            pltpu.VMEM((2, NT * 8, 128), f32),
-            pltpu.VMEM((NZ, NT, ROWS), f32),
-            pltpu.VMEM((NZ, NT, ROWS), f32),
-            pltpu.VMEM((NZ, 2, 8, 128), f32),
-            pltpu.VMEM((2, NZ * 8, 128), f32),
-            pltpu.VMEM((8, 8, ROWS), f32),
-            pltpu.VMEM((NVEC, 2 * ROWS), f32),
+            pltpu.VMEM((2, 2, 128, 128), f32),
+            pltpu.VMEM((2, NZ, 16, ROWS), f32),
+            pltpu.VMEM((2, NZ, 16, ROWS), f32),
+            pltpu.VMEM((2, 16, ROWS), f32),
+            pltpu.VMEM((NF, 2, 128), f32),
+            pltpu.VMEM((NF, 2, 128), f32),
             dma((6,)),
             dma((9,)), dma((9,)), dma((8,)), dma((8,)),
             dma((8,)), dma((8,)), dma, dma,
             dma((4,)), dma((4,)),
-            dma((8,)), dma((8,)), dma((8,)), dma((8,)), dma((8,)), dma((8,)),
+            dma((2, 8)), dma((2, 8)), dma, dma,
         ],
         compiler_params=pltpu.CompilerParams(collective_id=0, has_side_effects=True),
     )(

time: 54.9 us -> 53.8 us (0.980)
  Pallas kernels: 53.1 us -> 52.1 us
    pallas_call x1, Pallas kernels: 53.1 us -> 52.1 us  [shards(): pl.pallas_call(kernel, out_shape=jax.ShapeDtypeStruct((1, NVEC, occ.shape...]
where the time goes in v2:
time: 53.8 us; the launch traced here: 53.6 us
  Pallas kernels  52.1 us (97%)
  local copies, waits for them, and re-layouts  1.47 us (3%)
    pallas_call x1, Pallas kernels, shards(): pl.pallas_call(kernel, out_shape=jax.ShapeDtypeStruct((1, NVEC, occ.shape...  52.1 us
    unnamed x1, local copies, waits for them, and re-layouts  1.47 us

profile of v2, /device:TPU:1, one launch (start us, length us, event | category | flops | bytes accessed | tf_op | source)
XLA Modules:
  0.0 53.6 jit_solution(10457263838814938145)
XLA Ops:
  0.0 52.1 %shard_map.82 = f32[1,32,512]{2,1,0:T(8,128)} custom-call(bf16[512,512]{1,0:T(8,128)(2,1)} %occ_hbm.1, bf16[512,1536]{1,0:T(8,128)(2,1)} %virt_hbm.1, f32[1,512]{1,0:T(1,128)} %bitcast.5, f32[12,128]{1,0:T(8,128)} %bitcast.3, s32[8,32]{1,0:T(8,128)} %bitcast.4, bf16[32,64]{1,0:T(8,128)(2,1)} %probe_ref.1, f32[32,1]{1,0:T(8,128)} %constant.6.times_ref, ...), custom_call_target="tpu_custom_call" | custom-call | tf_op jit(solution)/shard_map/pallas_call | solution.py:345
  52.1 1.5 %copy.10 = f32[1,32,512]{2,1,0:T(8,128)} copy(f32[1,32,512]{2,1,0:T(8,128)} %shard_map.82) | data formatting | bytes 131072

commit v3 on v2

--- a/solution.py
+++ b/solution.py
@@ -37,10 +37,11 @@
 
 
 def kernel(
-    occ_hbm, virt_hbm, ogap_ref, vgap_ref, tiles_ref, probe_ref, times_ref, table_ref, out_ref,
+    occ_hbm, virt_hbm, ogap_hbm, vgap_hbm, tiles_hbm, probe_hbm, times_hbm, table_hbm, out_ref,
+    ogap_ref, vgap_ref, tiles_ref, probe_ref, times_ref, table_ref,
     points, r_occ, r_virt, weights, s_occ, s_virt, polar, padded, probes, picked_out, picked_in, left,
     keep, x1_out, x1_in, x2_out, x2_in, sums, zs_out, zs_in, zs_sum, trans, arrivals,
-    local_sem, y_send, y_recv, f_send, f_recv, p_send, p_recv, ps_send, ps_recv,
+    local_sem, y_send, y_recv, last_send, last_recv, f_send, f_recv, p_send, p_recv, ps_send, ps_recv,
     x_send, x_recv, zs_send, zs_recv, out_send, out_recv,
 ):
     ta = lax.axis_index("ta")
@@ -62,6 +63,7 @@
     partners = (at(z, near * 2 + c, y), at(z, far * 2 + c, y))
     greeted = [sibling, *partners]
     greeted += [at(z, e, lax.rem(y + d, NY)) for d in (1, 2, 6, 7)]
+    greeted += [at(z, x * 2 + 1 - c, lax.rem(y + d, NY)) for d in (2, 6)]
     greeted += [at(lax.rem(z + d, NZ), e, y) for d in range(1, NZ)]
     for who in greeted:
         pl.semaphore_signal(barrier, inc=1, device_id=who, device_id_type=MESH)
@@ -83,10 +85,15 @@
         pltpu.make_async_copy(occ_hbm.at[pl.ds(row0, ROWS), :], r_occ, local_sem.at[4]),
         pltpu.make_async_copy(virt_hbm.at[pl.ds(row0, ROWS), :], r_virt, local_sem.at[5]),
     ]
-    for copy in own_copies + row_copies:
+    small_copies = [
+        pltpu.make_async_copy(source, target, local_sem.at[6 + i])
+        for i, (source, target) in enumerate((
+            (probe_hbm, probe_ref), (times_hbm, times_ref), (ogap_hbm, ogap_ref),
+            (vgap_hbm, vgap_ref), (tiles_hbm, tiles_ref), (table_hbm, table_ref),
+        ))
+    ]
+    for copy in own_copies + small_copies + row_copies:
         copy.start()
-    padded[:, :64] = probe_ref[...]
-    padded[:, 64:] = jnp.zeros((NVEC, 64), jnp.bfloat16)
     for copy in own_copies:
         copy.wait()
     pl.semaphore_wait(barrier, len(greeted))
@@ -102,16 +109,31 @@
         sends.append(copy)
         return copy
 
-    def along_y(source, target, step, sem, part=slice(None)):
+    def along_y(source, target, step, sem):
         return remote(
-            points.at[source, c, :, part], points.at[target, c, :, part], y_send.at[sem],
-            y_recv.at[sem], at(z, e, lax.rem(y + step + NY, NY)),
-        )
+            points.at[source, c], points.at[target, c], y_send.at[sem], y_recv.at[sem],
+            at(z, e, lax.rem(y + step + NY, NY)),
+        )
+
+    def to_both(source, step, part, sem):
+        y_to = lax.rem(y + step + NY, NY)
+        copies = []
+        for other in range(2):
+            copies.append(remote(
+                points.at[source, c, :, part], points.at[4, c, :, part],
+                last_send.at[sem, other], last_recv.at[sem, other],
+                at(z, x * 2 + lax.rem(c + other, 2), y_to),
+            ))
+        return copies
 
     gathers = {
         2: along_y(0, 2, -2, 2), 6: along_y(0, 6, 2, 6), 1: along_y(0, 1, -1, 1),
         7: along_y(0, 7, 1, 7),
     }
+    for copy in small_copies:
+        copy.wait()
+    padded[:, :64] = probe_ref[...]
+    padded[:, 64:] = jnp.zeros((NVEC, 64), jnp.bfloat16)
     probe_copies = []
     for d in range(1, 8):
         probe_copies.append(
@@ -181,10 +203,10 @@
     quarter = (h_occ + h_virt) // 2
     gathers[2].wait_recv()
     gathers[3] = along_y(2, 3, -1, 3)
-    gathers[4] = along_y(2, 4, -2, 4, slice(0, quarter))
+    last = to_both(2, -2, slice(0, quarter), 0)
     gathers[6].wait_recv()
     gathers[5] = along_y(6, 5, 1, 5)
-    gathers[8] = along_y(6, 4, 2, 8, slice(quarter, 2 * quarter))
+    last += to_both(6, 2, slice(quarter, 2 * quarter), 1)
     for d in (2, 6):
         forward(d)
     for d in (1, 7):
@@ -196,9 +218,6 @@
         forward(d)
     both(7)
     both(2)
-    gathers[4].wait_recv()
-    gathers[8].wait_recv()
-    forward(4)
 
     for copy in probe_copies:
         copy.wait_recv()
@@ -239,7 +258,8 @@
         )
 
     exchanges = []
-    siblings[4].wait_recv()
+    for copy in last:
+        copy.wait_recv()
     for half in range(2):
         chunk(4, half)
         for t in range(16):
@@ -305,15 +325,21 @@
     for side in range(2):
         trans[:, side, :] = result[:, side * 128:(side + 1) * 128]
 
-    def hand_out(step, carry):
-        to = lax.rem(ta + step, NF)
-        pltpu.make_async_remote_copy(
-            src_ref=trans.at[to], dst_ref=arrivals.at[ta], send_sem=out_send, recv_sem=out_recv,
-            device_id=(to, y), device_id_type=MESH,
-        ).start()
+    def hand_out(i, carry):
+        place = i // 8
+        away = jnp.where(place % 2 == 0, 4 - place // 2, 4 + (place + 1) // 2)
+        to = lax.rem(z + away, NZ) * 8 + lax.rem(e + 4 + i % 8, 8)
+
+        @pl.when(to != ta)
+        def _():
+            pltpu.make_async_remote_copy(
+                src_ref=trans.at[to], dst_ref=arrivals.at[ta], send_sem=out_send,
+                recv_sem=out_recv, device_id=(to, y), device_id_type=MESH,
+            ).start()
+
         return carry
 
-    lax.fori_loop(1, NF, hand_out, 0)
+    lax.fori_loop(0, NF, hand_out, 0)
     arrivals[ta] = trans[ta]
     everything = pltpu.make_async_remote_copy(
         src_ref=trans.at[0:NF - 1], dst_ref=arrivals.at[0:NF - 1], send_sem=out_send,
@@ -344,10 +370,16 @@
     hbm = pl.BlockSpec(memory_space=pl.ANY)
     return pl.pallas_call(
         kernel,
-        out_shape=jax.ShapeDtypeStruct((1, NVEC, occ.shape[0]), f32),
-        in_specs=[hbm, hbm, vmem, vmem, vmem, vmem, vmem, vmem],
+        out_shape=pltpu.VMEM((1, NVEC, occ.shape[0]), f32),
+        in_specs=[hbm] * 8,
         out_specs=vmem,
         scratch_shapes=[
+            pltpu.VMEM((1, n_occ), f32),
+            pltpu.VMEM((n_virt // 128, 128), f32),
+            pltpu.VMEM(tiles.shape[::-1], jnp.int32),
+            pltpu.VMEM(probe.shape, bf16),
+            pltpu.VMEM((NT, 1), f32),
+            pltpu.VMEM((NF, NT), f32),
             pltpu.VMEM((NY, 2, COLS, n_all // 2), bf16),
             pltpu.VMEM((ROWS, n_occ), bf16),
             pltpu.VMEM((ROWS, n_virt), bf16),
@@ -371,8 +403,8 @@
             pltpu.VMEM((2, 16, ROWS), f32),
             pltpu.VMEM((NF, 2, 128), f32),
             pltpu.VMEM((NF, 2, 128), f32),
-            dma((6,)),
-            dma((9,)), dma((9,)), dma((8,)), dma((8,)),
+            dma((12,)),
+            dma((8,)), dma((8,)), dma((2, 2)), dma((2, 2)), dma((8,)), dma((8,)),
             dma((8,)), dma((8,)), dma, dma,
             dma((4,)), dma((4,)),
             dma((2, 8)), dma((2, 8)), dma, dma,

time: 53.8 us -> 52.7 us (0.980)
  local copies, waits for them, and re-layouts: 1.47 us -> 0.63 us
    unnamed x1, local copies, waits for them, and re-layouts: 1.47 us -> 0.63 us
where the time goes in v3:
time: 52.7 us; the launch traced here: 52.5 us
  Pallas kernels  51.9 us (98%)
  local copies, waits for them, and re-layouts  0.63 us (1%)
    pallas_call x1, Pallas kernels, shards(): pl.pallas_call(kernel, out_shape=pltpu.VMEM((1, NVEC, occ.shape[0]), f32)...  51.9 us

profile of v3, /device:TPU:1, one launch (start us, length us, event | category | flops | bytes accessed | tf_op | source)
XLA Modules:
  0.0 52.5 jit_solution(656998105860400049)
XLA Ops:
  0.0 51.9 %shard_map.82 = f32[1,32,512]{2,1,0:T(8,128)S(1)} custom-call(bf16[512,512]{1,0:T(8,128)(2,1)} %occ_hbm.1, bf16[512,1536]{1,0:T(8,128)(2,1)} %virt_hbm.1, f32[1,512]{1,0:T(1,128)} %bitcast.5, f32[12,128]{1,0:T(8,128)} %bitcast.3, s32[8,32]{1,0:T(8,128)} %bitcast.4, bf16[32,64]{1,0:T(8,128)(2,1)} %probe_hbm.1, f32[32,1]{1,0:T(8,128)} %constant.6.times_hbm, ...), custom_call_target="tpu_custom_call" | custom-call | tf_op jit(solution)/shard_map/pallas_call | solution.py:371
  51.9 0.6 %copy.10 = f32[1,32,512]{2,1,0:T(8,128)} copy(f32[1,32,512]{2,1,0:T(8,128)S(1)} %shard_map.82) | data formatting | bytes 131072

commit v4 on v3

--- a/solution.py
+++ b/solution.py
@@ -1,4 +1,4 @@
-import functools
+import itertools
 
 import jax
 import jax.numpy as jnp
@@ -109,9 +109,9 @@
         sends.append(copy)
         return copy
 
-    def along_y(source, target, step, sem):
+    def along_y(source, target, step, sem, part=c):
         return remote(
-            points.at[source, c], points.at[target, c], y_send.at[sem], y_recv.at[sem],
+            points.at[source, part], points.at[target, part], y_send.at[sem], y_recv.at[sem],
             at(z, e, lax.rem(y + step + NY, NY)),
         )
 
@@ -127,8 +127,8 @@
         return copies
 
     gathers = {
-        2: along_y(0, 2, -2, 2), 6: along_y(0, 6, 2, 6), 1: along_y(0, 1, -1, 1),
-        7: along_y(0, 7, 1, 7),
+        2: along_y(0, 2, -2, 2), 6: along_y(0, 6, 2, 6),
+        1: along_y(0, 1, -1, 1, pl.ds(0, 2)), 7: along_y(0, 7, 1, 7, pl.ds(0, 2)),
     }
     for copy in small_copies:
         copy.wait()
@@ -155,7 +155,10 @@
     for copy in row_copies:
         copy.wait()
 
+    turns = itertools.cycle(range(2))
+
     def chunk(d, t_half):
+        turn = next(turns)
         column_block = lax.rem(y + d, NY) * 4 + x
         hit = jnp.max(jnp.where(tiles == column_block, 1.0, 0.0), axis=0, keepdims=True)
         first_hit = jnp.sum(jnp.where(lane32 == row_block, hit, 0.0), axis=1, keepdims=True)
@@ -168,18 +171,18 @@
             virt_lanes = slice(h * h_virt, (h + 1) * h_virt)
             for t in range(16):
                 row = t_half * 16 + t
-                s_occ[t_half, t * COLS:(t + 1) * COLS, occ_lanes] = (
+                s_occ[turn, t * COLS:(t + 1) * COLS, occ_lanes] = (
                     xo * weights[row:row + 1, occ_lanes]
                 ).astype(jnp.bfloat16)
-                s_virt[t_half, t * COLS:(t + 1) * COLS, virt_lanes] = (
+                s_virt[turn, t * COLS:(t + 1) * COLS, virt_lanes] = (
                     xv * weights[row:row + 1, n_occ + h * h_virt:n_occ + (h + 1) * h_virt]
                 ).astype(jnp.bfloat16)
         dims = (((1,), (1,)), ((), ()))
         green_occ = lax.dot_general(
-            s_occ[t_half], r_occ[...], dims, preferred_element_type=jnp.float32
+            s_occ[turn], r_occ[...], dims, preferred_element_type=jnp.float32
         )
         green_virt = lax.dot_general(
-            s_virt[t_half], r_virt[...], dims, preferred_element_type=jnp.float32
+            s_virt[turn], r_virt[...], dims, preferred_element_type=jnp.float32
         )
         value = (green_occ * green_virt * mask).astype(jnp.bfloat16)
         polar[t_half * 16:(t_half + 1) * 16, d * COLS:(d + 1) * COLS, :] = value.reshape(
@@ -192,11 +195,6 @@
         siblings[d] = remote(
             points.at[d, c], points.at[d, c], f_send.at[d], f_recv.at[d], sibling
         )
-
-    def both(d):
-        siblings[d].wait_recv()
-        chunk(d, 0)
-        chunk(d, 1)
 
     chunk(0, 0)
     chunk(0, 1)
@@ -211,13 +209,14 @@
         forward(d)
     for d in (1, 7):
         gathers[d].wait_recv()
-        forward(d)
-    both(1)
+        chunk(d, 0)
+        chunk(d, 1)
     for d in (3, 5):
         gathers[d].wait_recv()
         forward(d)
-    both(7)
-    both(2)
+    for d in (2, 6):
+        siblings[d].wait_recv()
+        chunk(d, 0)
 
     for copy in probe_copies:
         copy.wait_recv()
@@ -231,9 +230,9 @@
         gathered += jnp.dot(probes[q], pick, preferred_element_type=jnp.float32)
     picked_out[...] = gathered.astype(jnp.bfloat16)
     probe_forward = remote(picked_out, picked_in, ps_send, ps_recv, sibling)
-    both(6)
-    both(3)
-    both(5)
+    for d in (3, 5):
+        siblings[d].wait_recv()
+        chunk(d, 0)
     probe_forward.wait_recv()
     gathered = jnp.where(
         z // 4 == c, picked_out[...].astype(jnp.float32), picked_in[...].astype(jnp.float32)
@@ -257,65 +256,92 @@
             jnp.bfloat16
         )
 
-    exchanges = []
     for copy in last:
         copy.wait_recv()
-    for half in range(2):
-        chunk(4, half)
-        for t in range(16):
+    chunk(4, 0)
+
+    exchanges = []
+
+    def first_exchange(part):
+        for i in range(8):
             terms = jnp.dot(
-                left[half], polar[half * 16 + t], preferred_element_type=jnp.float32
+                left[part % 2], polar[part * 8 + i], preferred_element_type=jnp.float32
             )
-            x1_out[half, t * 16:(t + 1) * 16, :] = terms[:16].astype(LINK)
-            keep[half, t] = terms[16:]
+            x1_out[part, i * 16:(i + 1) * 16, :] = terms[:16].astype(LINK)
+            keep[part, i] = terms[16:]
         exchanges.append(
-            remote(x1_out.at[half], x1_in.at[half], x_send.at[half], x_recv.at[half],
-                   partners[half])
-        )
+            remote(x1_out.at[part], x1_in.at[part], x_send.at[part], x_recv.at[part],
+                   partners[part % 2])
+        )
+
     seconds = []
-    for half in range(2):
-        exchanges[half].wait_recv()
-        for t in range(16):
-            total = keep[half, t] + x1_in[half, t * 16:(t + 1) * 16, :].astype(jnp.float32)
-            x2_out[half, t * 8:(t + 1) * 8, :] = total[:8].astype(LINK)
+
+    def second_exchange(part):
+        exchanges[part].wait_recv()
+        for i in range(8):
+            total = keep[part, i] + x1_in[part, i * 16:(i + 1) * 16, :].astype(jnp.float32)
+            x2_out[part, i * 8:(i + 1) * 8, :] = total[:8].astype(LINK)
             for side in range(2):
-                sums[side, half, t * 8:(t + 1) * 8, :] = total[8:, side * 128:(side + 1) * 128]
+                sums[side, part, i * 8:(i + 1) * 8, :] = total[8:, side * 128:(side + 1) * 128]
         seconds.append(
-            remote(x2_out.at[half], x2_in.at[half], x_send.at[2 + half], x_recv.at[2 + half],
-                   partners[1 - half])
-        )
-
-    def along_z(half, source, target, step, sem):
-        return remote(source, target, zs_send.at[half, sem], zs_recv.at[half, sem],
+            remote(x2_out.at[part], x2_in.at[part], x_send.at[4 + part], x_recv.at[4 + part],
+                   partners[1 - part % 2])
+        )
+
+    def along_z(part, source, target, step, sem):
+        return remote(source, target, zs_send.at[part, sem], zs_recv.at[part, sem],
                       at(lax.rem(z + step + NZ, NZ), e, y))
 
-    reduces, relays = [{}, {}], []
-    for half, sign in enumerate((1, -1)):
-        seconds[half].wait_recv()
-        arrived = x2_in[half].astype(jnp.float32)
+    reduces, relays = [{} for _ in range(4)], []
+
+    def start_z(part):
+        sign = 1 - 2 * (part % 2)
+        seconds[part].wait_recv()
+        arrived = x2_in[part].astype(jnp.float32)
         for side in range(2):
             lanes = slice(side * 128, (side + 1) * 128)
-            sums[side, half] += arrived[:, lanes]
+            sums[side, part] += arrived[:, lanes]
             for s in range(NZ):
-                zs_out[half, s, :, lanes] = sums[side, half, pl.ds(s, 16, stride=8), :]
+                zs_out[part, s, :, lanes] = sums[side, part, pl.ds(s, 8, stride=8), :]
         relays.append(
-            along_z(half, zs_out.at[half, lax.rem(z + 4, NZ)], zs_in.at[half, 4], sign, 4)
+            along_z(part, zs_out.at[part, lax.rem(z + 4, NZ)], zs_in.at[part, 4], sign, 4)
         )
         for d in (5, 2, 6, 1, 7):
-            reduces[half][d] = along_z(
-                half, zs_out.at[half, lax.rem(z + sign * d + NZ, NZ)], zs_in.at[half, d],
+            reduces[part][d] = along_z(
+                part, zs_out.at[part, lax.rem(z + sign * d + NZ, NZ)], zs_in.at[part, d],
                 sign * d, d,
             )
-    for half, sign in enumerate((1, -1)):
-        relays[half].wait_recv()
-        zs_sum[half] = zs_in[half, 4] + zs_out[half, lax.rem(z + sign * 3 + NZ, NZ)]
-        reduces[half][3] = along_z(half, zs_sum.at[half], zs_in.at[half, 3], sign * 3, 3)
+
+    def relay_z(part):
+        sign = 1 - 2 * (part % 2)
+        relays[part].wait_recv()
+        zs_sum[part] = zs_in[part, 4] + zs_out[part, lax.rem(z + sign * 3 + NZ, NZ)]
+        reduces[part][3] = along_z(part, zs_sum.at[part], zs_in.at[part, 3], sign * 3, 3)
+
+    first_exchange(0)
+    first_exchange(1)
+    for d in (2, 6, 3, 5, 4):
+        chunk(d, 1)
+    first_exchange(2)
+    first_exchange(3)
+    second_exchange(0)
+    second_exchange(1)
+    second_exchange(2)
+    second_exchange(3)
+    start_z(0)
+    start_z(1)
+    start_z(2)
+    relay_z(0)
+    start_z(3)
+    relay_z(1)
+    relay_z(2)
+    relay_z(3)
     totals = []
-    for half in range(2):
-        total = zs_out[half, z]
+    for part in range(4):
+        total = zs_out[part, z]
         for d in (7, 1, 6, 2, 5, 3):
-            reduces[half][d].wait_recv()
-            total += zs_in[half, d]
+            reduces[part][d].wait_recv()
+            total += zs_in[part, d]
         totals.append(total)
 
     result = jnp.dot(
@@ -392,22 +418,22 @@
             pltpu.VMEM((NVEC, CHIP_COLS), bf16),
             pltpu.VMEM((NVEC, CHIP_COLS), bf16),
             pltpu.VMEM((2, NVEC, CHIP_COLS), bf16),
-            pltpu.VMEM((2, 16, 16, ROWS), f32),
-            pltpu.VMEM((2, 256, ROWS), LINK),
-            pltpu.VMEM((2, 256, ROWS), LINK),
-            pltpu.VMEM((2, 128, ROWS), LINK),
-            pltpu.VMEM((2, 128, ROWS), LINK),
-            pltpu.VMEM((2, 2, 128, 128), f32),
-            pltpu.VMEM((2, NZ, 16, ROWS), f32),
-            pltpu.VMEM((2, NZ, 16, ROWS), f32),
-            pltpu.VMEM((2, 16, ROWS), f32),
+            pltpu.VMEM((4, 8, 16, ROWS), f32),
+            pltpu.VMEM((4, 128, ROWS), LINK),
+            pltpu.VMEM((4, 128, ROWS), LINK),
+            pltpu.VMEM((4, 64, ROWS), LINK),
+            pltpu.VMEM((4, 64, ROWS), LINK),
+            pltpu.VMEM((2, 4, 64, 128), f32),
+            pltpu.VMEM((4, NZ, 8, ROWS), f32),
+            pltpu.VMEM((4, NZ, 8, ROWS), f32),
+            pltpu.VMEM((4, 8, ROWS), f32),
             pltpu.VMEM((NF, 2, 128), f32),
             pltpu.VMEM((NF, 2, 128), f32),
             dma((12,)),
             dma((8,)), dma((8,)), dma((2, 2)), dma((2, 2)), dma((8,)), dma((8,)),
             dma((8,)), dma((8,)), dma, dma,
-            dma((4,)), dma((4,)),
-            dma((2, 8)), dma((2, 8)), dma, dma,
+            dma((8,)), dma((8,)),
+            dma((4, 8)), dma((4, 8)), dma, dma,
         ],
         compiler_params=pltpu.CompilerParams(collective_id=0, has_side_effects=True),
     )(

time: 52.7 us -> 52 us (0.987)
  Pallas kernels: 51.9 us -> 51.2 us
    pallas_call x1, Pallas kernels: 51.9 us -> 51.2 us  [shards(): pl.pallas_call(kernel, out_shape=pltpu.VMEM((1, NVEC, occ.shape[0]), f32)...]
where the time goes in v4:
time: 52 us; the launch traced here: 51.9 us
  Pallas kernels  51.2 us (98%)
  local copies, waits for them, and re-layouts  0.63 us (1%)
    pallas_call x1, Pallas kernels, shards(): pl.pallas_call(kernel, out_shape=pltpu.VMEM((1, NVEC, occ.shape[0]), f32)...  51.2 us

profile of v4, /device:TPU:1, one launch (start us, length us, event | category | flops | bytes accessed | tf_op | source)
XLA Modules:
  0.0 51.9 jit_solution(14008443656916207965)
XLA Ops:
  0.0 51.2 %shard_map.82 = f32[1,32,512]{2,1,0:T(8,128)S(1)} custom-call(bf16[512,512]{1,0:T(8,128)(2,1)} %occ_hbm.1, bf16[512,1536]{1,0:T(8,128)(2,1)} %virt_hbm.1, f32[1,512]{1,0:T(1,128)} %bitcast.5, f32[12,128]{1,0:T(8,128)} %bitcast.3, s32[8,32]{1,0:T(8,128)} %bitcast.4, bf16[32,64]{1,0:T(8,128)(2,1)} %probe_hbm.1, f32[32,1]{1,0:T(8,128)} %constant.6.times_hbm, ...), custom_call_target="tpu_custom_call" | custom-call | tf_op jit(solution)/shard_map/pallas_call | solution.py:397
  51.2 0.6 %copy.10 = f32[1,32,512]{2,1,0:T(8,128)} copy(f32[1,32,512]{2,1,0:T(8,128)S(1)} %shard_map.82) | data formatting | bytes 131072

commit v5 on v4

--- a/solution.py
+++ b/solution.py
@@ -109,9 +109,9 @@
         sends.append(copy)
         return copy
 
-    def along_y(source, target, step, sem, part=c):
+    def along_y(source, target, step, sem):
         return remote(
-            points.at[source, part], points.at[target, part], y_send.at[sem], y_recv.at[sem],
+            points.at[source, c], points.at[target, c], y_send.at[sem], y_recv.at[sem],
             at(z, e, lax.rem(y + step + NY, NY)),
         )
 
@@ -128,7 +128,7 @@
 
     gathers = {
         2: along_y(0, 2, -2, 2), 6: along_y(0, 6, 2, 6),
-        1: along_y(0, 1, -1, 1, pl.ds(0, 2)), 7: along_y(0, 7, 1, 7, pl.ds(0, 2)),
+        1: along_y(0, 1, -1, 1), 7: along_y(0, 7, 1, 7),
     }
     for copy in small_copies:
         copy.wait()
@@ -205,10 +205,13 @@
     gathers[6].wait_recv()
     gathers[5] = along_y(6, 5, 1, 5)
     last += to_both(6, 2, slice(quarter, 2 * quarter), 1)
+    for d in (1, 7):
+        gathers[d].wait_recv()
+        forward(d)
     for d in (2, 6):
         forward(d)
     for d in (1, 7):
-        gathers[d].wait_recv()
+        siblings[d].wait_recv()
         chunk(d, 0)
         chunk(d, 1)
     for d in (3, 5):
@@ -288,11 +291,14 @@
                    partners[1 - part % 2])
         )
 
-    def along_z(part, source, target, step, sem):
-        return remote(source, target, zs_send.at[part, sem], zs_recv.at[part, sem],
+    def along_z(part, source, step, sem):
+        return remote(source, zs_in.at[part, sem], zs_send.at[part, sem], zs_recv.at[part, sem],
                       at(lax.rem(z + step + NZ, NZ), e, y))
 
-    reduces, relays = [{} for _ in range(4)], []
+    hops = [{} for _ in range(4)]
+
+    def piece(part, distance):
+        return zs_out.at[part, lax.rem(z + distance + NZ, NZ)]
 
     def start_z(part):
         sign = 1 - 2 * (part % 2)
@@ -303,20 +309,20 @@
             sums[side, part] += arrived[:, lanes]
             for s in range(NZ):
                 zs_out[part, s, :, lanes] = sums[side, part, pl.ds(s, 8, stride=8), :]
-        relays.append(
-            along_z(part, zs_out.at[part, lax.rem(z + 4, NZ)], zs_in.at[part, 4], sign, 4)
-        )
-        for d in (5, 2, 6, 1, 7):
-            reduces[part][d] = along_z(
-                part, zs_out.at[part, lax.rem(z + sign * d + NZ, NZ)], zs_in.at[part, d],
-                sign * d, d,
-            )
-
-    def relay_z(part):
+        hops[part][0] = along_z(part, piece(part, 4), sign, 0)
+        hops[part][4] = along_z(part, piece(part, -3 * sign), -sign, 4)
+
+    def carry_on(part, step):
         sign = 1 - 2 * (part % 2)
-        relays[part].wait_recv()
-        zs_sum[part] = zs_in[part, 4] + zs_out[part, lax.rem(z + sign * 3 + NZ, NZ)]
-        reduces[part][3] = along_z(part, zs_sum.at[part], zs_in.at[part, 3], sign * 3, 3)
+        for first, sense, distance in ((0, sign, 4 - step), (4, -sign, 3 - step)):
+            if distance:
+                hops[part][first + step - 1].wait_recv()
+                zs_sum[part, first + step] = (
+                    zs_in[part, first + step - 1] + piece(part, sense * distance)[...]
+                )
+                hops[part][first + step] = along_z(
+                    part, zs_sum.at[part, first + step], sense, first + step
+                )
 
     first_exchange(0)
     first_exchange(1)
@@ -328,21 +334,16 @@
     second_exchange(1)
     second_exchange(2)
     second_exchange(3)
-    start_z(0)
-    start_z(1)
-    start_z(2)
-    relay_z(0)
-    start_z(3)
-    relay_z(1)
-    relay_z(2)
-    relay_z(3)
+    for part in range(4):
+        start_z(part)
+    for step in range(1, 4):
+        for part in range(4):
+            carry_on(part, step)
     totals = []
     for part in range(4):
-        total = zs_out[part, z]
-        for d in (7, 1, 6, 2, 5, 3):
-            reduces[part][d].wait_recv()
-            total += zs_in[part, d]
-        totals.append(total)
+        hops[part][3].wait_recv()
+        hops[part][6].wait_recv()
+        totals.append(zs_out[part, z] + zs_in[part, 3] + zs_in[part, 6])
 
     result = jnp.dot(
         table_ref[...], jnp.concatenate(totals, axis=0), preferred_element_type=jnp.float32,
@@ -426,7 +427,7 @@
             pltpu.VMEM((2, 4, 64, 128), f32),
             pltpu.VMEM((4, NZ, 8, ROWS), f32),
             pltpu.VMEM((4, NZ, 8, ROWS), f32),
-            pltpu.VMEM((4, 8, ROWS), f32),
+            pltpu.VMEM((4, 8, 8, ROWS), f32),
             pltpu.VMEM((NF, 2, 128), f32),
             pltpu.VMEM((NF, 2, 128), f32),
             dma((12,)),

time: 52 us -> 55.8 us (1.073)
  Pallas kernels: 51.2 us -> 55 us
    pallas_call x1, Pallas kernels: 51.2 us -> 55 us  [shards(): pl.pallas_call(kernel, out_shape=pltpu.VMEM((1, NVEC, occ.shape[0]), f32)...]
where the time goes in v5:
time: 55.8 us; the launch traced here: 55.7 us
  Pallas kernels  55 us (99%)
  local copies, waits for them, and re-layouts  0.63 us (1%)
    pallas_call x1, Pallas kernels, shards(): pl.pallas_call(kernel, out_shape=pltpu.VMEM((1, NVEC, occ.shape[0]), f32)...  55 us

profile of v5, /device:TPU:1, one launch (start us, length us, event | category | flops | bytes accessed | tf_op | source)
XLA Modules:
  0.0 55.7 jit_solution(6264881714564592804)
XLA Ops:
  0.0 55.0 %shard_map.82 = f32[1,32,512]{2,1,0:T(8,128)S(1)} custom-call(bf16[512,512]{1,0:T(8,128)(2,1)} %occ_hbm.1, bf16[512,1536]{1,0:T(8,128)(2,1)} %virt_hbm.1, f32[1,512]{1,0:T(1,128)} %bitcast.5, f32[12,128]{1,0:T(8,128)} %bitcast.3, s32[8,32]{1,0:T(8,128)} %bitcast.4, bf16[32,64]{1,0:T(8,128)(2,1)} %probe_hbm.1, f32[32,1]{1,0:T(8,128)} %constant.6.times_hbm, ...), custom_call_target="tpu_custom_call" | custom-call | tf_op jit(solution)/shard_map/pallas_call | solution.py:398
  55.0 0.6 %copy.10 = f32[1,32,512]{2,1,0:T(8,128)} copy(f32[1,32,512]{2,1,0:T(8,128)S(1)} %shard_map.82) | data formatting | bytes 131072

commit v6 on v5

--- a/solution.py
+++ b/solution.py
@@ -12,6 +12,7 @@
 NT = 32
 NVEC = 32
 NF = 64
+Z_GROUPS = 2
 BLK = 128
 NZ = 8
 NX = 4
@@ -40,7 +41,7 @@
     occ_hbm, virt_hbm, ogap_hbm, vgap_hbm, tiles_hbm, probe_hbm, times_hbm, table_hbm, out_ref,
     ogap_ref, vgap_ref, tiles_ref, probe_ref, times_ref, table_ref,
     points, r_occ, r_virt, weights, s_occ, s_virt, polar, padded, probes, picked_out, picked_in, left,
-    keep, x1_out, x1_in, x2_out, x2_in, sums, zs_out, zs_in, zs_sum, trans, arrivals,
+    keep, x1_out, x1_in, x2_out, x2_in, sums, zs_out, zs_in, trans, arrivals,
     local_sem, y_send, y_recv, last_send, last_recv, f_send, f_recv, p_send, p_recv, ps_send, ps_recv,
     x_send, x_recv, zs_send, zs_recv, out_send, out_recv,
 ):
@@ -291,38 +292,25 @@
                    partners[1 - part % 2])
         )
 
-    def along_z(part, source, step, sem):
-        return remote(source, zs_in.at[part, sem], zs_send.at[part, sem], zs_recv.at[part, sem],
-                      at(lax.rem(z + step + NZ, NZ), e, y))
-
-    hops = [{} for _ in range(4)]
-
-    def piece(part, distance):
-        return zs_out.at[part, lax.rem(z + distance + NZ, NZ)]
+    reduces = [{} for _ in range(Z_GROUPS)]
 
     def start_z(part):
-        sign = 1 - 2 * (part % 2)
+        group, row = divmod(part * 8, NT // Z_GROUPS)
         seconds[part].wait_recv()
         arrived = x2_in[part].astype(jnp.float32)
         for side in range(2):
             lanes = slice(side * 128, (side + 1) * 128)
             sums[side, part] += arrived[:, lanes]
             for s in range(NZ):
-                zs_out[part, s, :, lanes] = sums[side, part, pl.ds(s, 8, stride=8), :]
-        hops[part][0] = along_z(part, piece(part, 4), sign, 0)
-        hops[part][4] = along_z(part, piece(part, -3 * sign), -sign, 4)
-
-    def carry_on(part, step):
-        sign = 1 - 2 * (part % 2)
-        for first, sense, distance in ((0, sign, 4 - step), (4, -sign, 3 - step)):
-            if distance:
-                hops[part][first + step - 1].wait_recv()
-                zs_sum[part, first + step] = (
-                    zs_in[part, first + step - 1] + piece(part, sense * distance)[...]
-                )
-                hops[part][first + step] = along_z(
-                    part, zs_sum.at[part, first + step], sense, first + step
-                )
+                zs_out[group, s, row:row + 8, lanes] = sums[side, part, pl.ds(s, 8, stride=8), :]
+        if row + 8 < NT // Z_GROUPS:
+            return
+        for d in (4, 3, 5, 2, 6, 1, 7):
+            to = lax.rem(z + d, NZ)
+            reduces[group][d] = remote(
+                zs_out.at[group, to], zs_in.at[group, d], zs_send.at[group, d],
+                zs_recv.at[group, d], at(to, e, y),
+            )
 
     first_exchange(0)
     first_exchange(1)
@@ -332,18 +320,19 @@
     first_exchange(3)
     second_exchange(0)
     second_exchange(1)
+    start_z(0)
     second_exchange(2)
+    start_z(1)
     second_exchange(3)
-    for part in range(4):
-        start_z(part)
-    for step in range(1, 4):
-        for part in range(4):
-            carry_on(part, step)
+    start_z(2)
+    start_z(3)
     totals = []
-    for part in range(4):
-        hops[part][3].wait_recv()
-        hops[part][6].wait_recv()
-        totals.append(zs_out[part, z] + zs_in[part, 3] + zs_in[part, 6])
+    for group in range(Z_GROUPS):
+        total = zs_out[group, z]
+        for d in (7, 1, 6, 2, 5, 3, 4):
+            reduces[group][d].wait_recv()
+            total += zs_in[group, d]
+        totals.append(total)
 
     result = jnp.dot(
         table_ref[...], jnp.concatenate(totals, axis=0), preferred_element_type=jnp.float32,
@@ -352,21 +341,15 @@
     for side in range(2):
         trans[:, side, :] = result[:, side * 128:(side + 1) * 128]
 
-    def hand_out(i, carry):
-        place = i // 8
-        away = jnp.where(place % 2 == 0, 4 - place // 2, 4 + (place + 1) // 2)
-        to = lax.rem(z + away, NZ) * 8 + lax.rem(e + 4 + i % 8, 8)
-
-        @pl.when(to != ta)
-        def _():
-            pltpu.make_async_remote_copy(
-                src_ref=trans.at[to], dst_ref=arrivals.at[ta], send_sem=out_send,
-                recv_sem=out_recv, device_id=(to, y), device_id_type=MESH,
-            ).start()
-
-        return carry
-
-    lax.fori_loop(0, NF, hand_out, 0)
+    for dz in (4, 3, 5, 2, 6, 1, 7, 0):
+        z_to = lax.rem(z + dz, NZ) * 8
+        for de in (4, 5, 2, 3, 6, 7, 1, 0):
+            if dz or de:
+                to = z_to + lax.rem(e + de, 8)
+                pltpu.make_async_remote_copy(
+                    src_ref=trans.at[to], dst_ref=arrivals.at[ta], send_sem=out_send,
+                    recv_sem=out_recv, device_id=(to, y), device_id_type=MESH,
+                ).start()
     arrivals[ta] = trans[ta]
     everything = pltpu.make_async_remote_copy(
         src_ref=trans.at[0:NF - 1], dst_ref=arrivals.at[0:NF - 1], send_sem=out_send,
@@ -425,16 +408,15 @@
             pltpu.VMEM((4, 64, ROWS), LINK),
             pltpu.VMEM((4, 64, ROWS), LINK),
             pltpu.VMEM((2, 4, 64, 128), f32),
-            pltpu.VMEM((4, NZ, 8, ROWS), f32),
-            pltpu.VMEM((4, NZ, 8, ROWS), f32),
-            pltpu.VMEM((4, 8, 8, ROWS), f32),
+            pltpu.VMEM((Z_GROUPS, NZ, NT // Z_GROUPS, ROWS), f32),
+            pltpu.VMEM((Z_GROUPS, NZ, NT // Z_GROUPS, ROWS), f32),
             pltpu.VMEM((NF, 2, 128), f32),
             pltpu.VMEM((NF, 2, 128), f32),
             dma((12,)),
             dma((8,)), dma((8,)), dma((2, 2)), dma((2, 2)), dma((8,)), dma((8,)),
             dma((8,)), dma((8,)), dma, dma,
             dma((8,)), dma((8,)),
-            dma((4, 8)), dma((4, 8)), dma, dma,
+            dma((Z_GROUPS, 8)), dma((Z_GROUPS, 8)), dma, dma,
         ],
         compiler_params=pltpu.CompilerParams(collective_id=0, has_side_effects=True),
     )(

time: 55.8 us -> 49.9 us (0.89)
  Pallas kernels: 55 us -> 49.2 us
    pallas_call x1, Pallas kernels: 55 us -> 49.2 us  [shards(): pl.pallas_call(kernel, out_shape=pltpu.VMEM((1, NVEC, occ.shape[0]), f32)...]
where the time goes in v6:
time: 49.9 us; the launch traced here: 49.8 us
  Pallas kernels  49.2 us (99%)
  local copies, waits for them, and re-layouts  0.63 us (1%)
    pallas_call x1, Pallas kernels, shards(): pl.pallas_call(kernel, out_shape=pltpu.VMEM((1, NVEC, occ.shape[0]), f32)...  49.2 us

profile of v6, /device:TPU:1, one launch (start us, length us, event | category | flops | bytes accessed | tf_op | source)
XLA Modules:
  0.0 49.8 jit_solution(6871693243084246089)
XLA Ops:
  0.0 49.2 %shard_map.82 = f32[1,32,512]{2,1,0:T(8,128)S(1)} custom-call(bf16[512,512]{1,0:T(8,128)(2,1)} %occ_hbm.1, bf16[512,1536]{1,0:T(8,128)(2,1)} %virt_hbm.1, f32[1,512]{1,0:T(1,128)} %bitcast.5, f32[12,128]{1,0:T(8,128)} %bitcast.3, s32[8,32]{1,0:T(8,128)} %bitcast.4, bf16[32,64]{1,0:T(8,128)(2,1)} %probe_hbm.1, f32[32,1]{1,0:T(8,128)} %constant.6.times_hbm, ...), custom_call_target="tpu_custom_call" | custom-call | tf_op jit(solution)/shard_map/pallas_call | solution.py:381
  49.2 0.6 %copy.10 = f32[1,32,512]{2,1,0:T(8,128)} copy(f32[1,32,512]{2,1,0:T(8,128)S(1)} %shard_map.82) | data formatting | bytes 131072

commit v7 on v6

--- a/solution.py
+++ b/solution.py
@@ -221,6 +221,7 @@
     for d in (2, 6):
         siblings[d].wait_recv()
         chunk(d, 0)
+        chunk(d, 1)
 
     for copy in probe_copies:
         copy.wait_recv()
@@ -237,6 +238,7 @@
     for d in (3, 5):
         siblings[d].wait_recv()
         chunk(d, 0)
+        chunk(d, 1)
     probe_forward.wait_recv()
     gathered = jnp.where(
         z // 4 == c, picked_out[...].astype(jnp.float32), picked_in[...].astype(jnp.float32)
@@ -314,8 +316,7 @@
 
     first_exchange(0)
     first_exchange(1)
-    for d in (2, 6, 3, 5, 4):
-        chunk(d, 1)
+    chunk(4, 1)
     first_exchange(2)
     first_exchange(3)
     second_exchange(0)
@@ -355,6 +356,8 @@
         src_ref=trans.at[0:NF - 1], dst_ref=arrivals.at[0:NF - 1], send_sem=out_send,
         recv_sem=out_recv, device_id=sibling, device_id_type=MESH,
     )
+    for copy in sends:
+        copy.wait_send()
     everything.wait_recv()
     for x_from in range(NX):
         block = (0, 2, 3, 1)[x_from]
@@ -366,8 +369,6 @@
                         z_from * 8 + x_from * 2 + c_from, side
                     ]
     everything.wait_send()
-    for copy in sends:
-        copy.wait_send()
 
 
 def shards(occ, virt, ogap, vgap, tiles, probe):

time: 49.9 us -> 51.1 us (1.024)
  Pallas kernels: 49.2 us -> 50.3 us
    pallas_call x1, Pallas kernels: 49.2 us -> 50.3 us  [shards(): pl.pallas_call(kernel, out_shape=pltpu.VMEM((1, NVEC, occ.shape[0]), f32)...]
where the time goes in v7:
time: 51.1 us; the launch traced here: 51 us
  Pallas kernels  50.3 us (98%)
  local copies, waits for them, and re-layouts  0.63 us (1%)
    pallas_call x1, Pallas kernels, shards(): pl.pallas_call(kernel, out_shape=pltpu.VMEM((1, NVEC, occ.shape[0]), f32)...  50.3 us

profile of v7, /device:TPU:1, one launch (start us, length us, event | category | flops | bytes accessed | tf_op | source)
XLA Modules:
  0.0 51.0 jit_solution(16812694427282064527)
XLA Ops:
  0.0 50.3 %shard_map.82 = f32[1,32,512]{2,1,0:T(8,128)S(1)} custom-call(bf16[512,512]{1,0:T(8,128)(2,1)} %occ_hbm.1, bf16[512,1536]{1,0:T(8,128)(2,1)} %virt_hbm.1, f32[1,512]{1,0:T(1,128)} %bitcast.5, f32[12,128]{1,0:T(8,128)} %bitcast.3, s32[8,32]{1,0:T(8,128)} %bitcast.4, bf16[32,64]{1,0:T(8,128)(2,1)} %probe_hbm.1, f32[32,1]{1,0:T(8,128)} %constant.6.times_hbm, ...), custom_call_target="tpu_custom_call" | custom-call | tf_op jit(solution)/shard_map/pallas_call | solution.py:382
  50.3 0.6 %copy.10 = f32[1,32,512]{2,1,0:T(8,128)} copy(f32[1,32,512]{2,1,0:T(8,128)S(1)} %shard_map.82) | data formatting | bytes 131072
